TPU v7x, 512 devices: a whole 4x4x16 slice. The times are simulated.
512 devices in a mesh: segment: 64 (over z, y_lo, core), rows: 8 (over x, y_hi).
Axes of the slice: x: 4, y: 4 (y_hi: 2, y_lo: 2; y = y_hi * 2 + y_lo), z: 16, core: 2. Of those that a mesh axis runs over, the one named last changes fastest.
Arguments:
- encoder_weight: bfloat16 [64, 3, 3, 384, 384], P('segment', None, None, 'rows'), may hold values from -0.109375 to 0.109375
- encoder_bias: float32 [64, 384], P('segment'), may hold values from -3 to 3
- decoder_weight: bfloat16 [64, 3, 3, 768, 384], P('segment', None, None, 'rows'), may hold values from -0.078125 to 0.078125
- decoder_bias: float32 [64, 384], P('segment'), may hold values from -3 to 3
- encoder_inputs: bfloat16 [64, 1, 24, 64, 384], P('segment', None, 'rows'), may hold values from -6 to 6
- decoder_inputs: bfloat16 [64, 1, 24, 64, 384], P('segment', None, 'rows'), may hold values from -6 to 6
- arrivals: bfloat16 [3, 1, 24, 64, 384], P(None, None, 'rows'), may hold values from -6 to 6
- skip_buffer: bfloat16 [64, 4, 1, 24, 64, 384], P('segment', None, None, 'rows'), may hold values from -6 to 6
Outputs:
- encoder_results: bfloat16 [64, 4, 1, 24, 64, 384], P('segment', None, None, 'rows')
- decoder_results: bfloat16 [64, 4, 1, 24, 64, 384], P('segment', None, None, 'rows')
All inputs are finite; a program needn't handle non-finite values.
Results may differ from a plain program's by a relative error of at most 0.0036.
Values may be sent and summed in bfloat16 or wider, within the bound.
No kernel may reach another device: no remote copies, remote signals or barrier semaphores. Data moves between devices by JAX's collectives and lax.ppermute only.
A program may use at most 64 MiB of HBM per device.

v0:
```python
import jax
import jax.numpy as jnp
from jax import lax
from jax.experimental import pallas as pl
from jax.experimental.pallas import tpu as pltpu
from jax.sharding import PartitionSpec as P


AXES = ("segment", "rows")
BF = jnp.bfloat16
F32 = jnp.float32
TAPS = 9
LIMIT = 24 * 2**20


def call(arrays, outs, body, scratch=(), flops=0, where=()):
    names = list(arrays)
    arrays = {
        n: pltpu.with_memory_space_constraint(a, pltpu.HBM) if dict(where).get(n) == "hbm" else a
        for n, a in arrays.items()
    }

    def kernel(*refs):
        ins = dict(zip(names, refs))
        rest = refs[len(names) :]
        body(ins, rest[: len(outs)], rest[len(outs) :])

    spaces = {None: pltpu.VMEM, "any": pl.ANY, "hbm": pltpu.HBM}
    vmem = pl.BlockSpec(memory_space=pltpu.VMEM)
    shapes = [jax.ShapeDtypeStruct(s, d) for s, d in outs]
    nbytes = sum(a.size * a.dtype.itemsize for a in arrays.values())
    return pl.pallas_call(
        kernel,
        out_shape=shapes,
        in_specs=[pl.BlockSpec(memory_space=spaces[dict(where).get(n)]) for n in names],
        out_specs=[vmem] * len(outs),
        scratch_shapes=list(scratch),
        compiler_params=pltpu.CompilerParams(vmem_limit_bytes=LIMIT),
        cost_estimate=pl.CostEstimate(flops=flops, bytes_accessed=nbytes, transcendentals=0),
    )(*arrays.values())


def put(ref, views):
    at = 0
    for view in views:
        if isinstance(view, int):
            at += view
            continue
        if len(view.shape) == 2:
            view = view[...].reshape((-1,) + ref.shape[1:])
        ref[at : at + view.shape[0]] = view[...]
        at += view.shape[0]


def fill(x_ref, cases, own, total):
    for when, views in cases:
        pl.when(when)(lambda views=views: put(x_ref, views))
    count = x_ref.shape[0]
    rim = (count - own) // 2
    first = lax.axis_index("rows") * own - rim
    for i in list(range(rim)) + list(range(count - rim, count)):

        @pl.when((first + i < 0) | (first + i >= total))
        def _():
            x_ref[i] = jnp.zeros(x_ref.shape[1:], x_ref.dtype)


def patches(x_ref):
    rows, (width, channels) = x_ref.shape[0] - 2, x_ref.shape[1:]
    parts = [x_ref[t : t + rows].reshape(rows * width, channels) for t in range(3)]
    return jnp.concatenate(parts, axis=1)


def products(left, w_refs, y_ref):
    for column in range(3):
        right = jnp.concatenate([w[3 * t + column] for w in w_refs for t in range(3)], axis=0)
        y_ref[column] = jnp.dot(left, right, preferred_element_type=F32)


def combine(y_ref, row, width):
    span = pl.ds(row * width, width)
    place = lax.broadcasted_iota(jnp.int32, (width, y_ref.shape[2]), 0)
    before = jnp.where(place == 0, 0.0, pltpu.roll(y_ref[0, span], 1, 0))
    after = jnp.where(place == width - 1, 0.0, pltpu.roll(y_ref[2, span], width - 1, 0))
    return y_ref[1, span] + before + after


def finish(x_refs, w_refs, y_ref, bias_ref, ready, acc_ref, store):
    rows, width = x_refs[0].shape[0] - 2, x_refs[0].shape[1]
    left = [patches(x) for x in x_refs]
    left = left[0] if len(left) == 1 else jnp.concatenate(left, axis=1)
    products(left, w_refs, y_ref)
    ready.wait()
    bias = bias_ref[...]
    for row in range(rows):
        v = combine(y_ref, row, width) + bias
        if acc_ref is not None:
            v = v + acc_ref[row]
        store(row, (v / (1.0 + jnp.exp(-v))).astype(BF))


def sources(ring):
    block = lax.axis_index("rows")
    near = [block, lax.rem(block + ring - 2, ring), lax.rem(block + 2, ring)]
    far = lax.rem(block + 4, ring)
    swap = lambda r: r + 1 - 2 * lax.rem(r, 2)
    return near + [swap(block), far, swap(near[1]), swap(near[2]), swap(far)]


def shards(
    encoder_weight,
    encoder_bias,
    decoder_weight,
    decoder_bias,
    encoder_inputs,
    decoder_inputs,
    arrivals,
    skip_buffer,
):
    segments = lax.axis_size("segment")
    ring = lax.axis_size("rows")
    own, width, channels = encoder_inputs.shape[2:]
    outs = encoder_weight.shape[4]
    total = own * ring

    def pairs(move):
        found = []
        for s in range(segments):
            for r in range(ring):
                ts, tr = move(s, r)
                if 0 <= ts < segments and 0 <= tr < ring:
                    found.append((s * ring + r, ts * ring + tr))
        return found

    ahead = pairs(lambda s, r: (s, (r + 2) % ring))
    behind = pairs(lambda s, r: (s, (r - 2) % ring))
    opposite = pairs(lambda s, r: (s, (r + 4) % ring))
    across = pairs(lambda s, r: (s, r ^ 1))
    step = lambda r: r + 1 if r % 2 else r - 1
    cross = pairs(lambda s, r: (s, step(r)))
    first_across = pairs(lambda s, r: (s, r ^ 1 if s == 0 else -1))
    first_cross = pairs(lambda s, r: (s, step(r) if s == 0 else -1))
    up = pairs(lambda s, r: (s + 1, r))
    down = pairs(lambda s, r: (s - 1, r))
    down_after = pairs(lambda s, r: (s - 1, r + 1))
    down_before = pairs(lambda s, r: (s - 1, r - 1))

    def send(value, route):
        return lax.ppermute(value, AXES, route)

    enc_in = encoder_inputs[0, 0]
    dec_in = decoder_inputs[0, 0]
    skip = skip_buffer[0, :, 0]
    arr = arrivals[:, 0]
    image = (width, channels)

    e_own = encoder_weight.reshape(TAPS, -1, outs)
    d_own = decoder_weight.reshape(TAPS, -1, outs)
    ke, kd = e_own.shape[1], d_own.shape[1]

    ne = TAPS * ke

    ne = TAPS * ke
    extra = -(-width // ke)

    depth = [3, 2, 2, 1, 2, 1]
    arr_depth = [3, 2, 1]
    starts = [sum(depth[:i]) for i in range(len(depth) + 1)]
    arr_starts = [sum(arr_depth[:i]) for i in range(len(arr_depth) + 1)]


    chunks = [(n, n * ke, min(width, (n + 1) * ke)) for n in range(extra)]

    def pack(ins, out, scratch):
        sems = scratch[0]
        even = lax.rem(lax.axis_index("rows"), 2) == 0
        rows = [ins["enc"], ins["dec"]] + [ins["skip"].at[t] for t in range(4)]
        arrs = [ins["arr"].at[t] for t in range(3)]
        jobs = []
        for first, second, group, sizes in (
            (out[0], out[1], rows, depth),
            (out[2], out[3], arrs, arr_depth),
        ):
            at = 0
            for a, n in zip(group, sizes):
                last, head = a.at[own - n : own], a.at[0:n]
                to = [o.at[at : at + n] for o in (first, second)]
                jobs.append(((last, to[0]), (head, to[0])))
                jobs.append(((head, to[1]), (last, to[1])))
                at += n
        for o, row in ((out[4], own - 1), (out[5], 0)):
            jobs.append(((ins["e"], o.at[:TAPS]),) * 2)
            for n, low, high in chunks:
                jobs.append(((ins["enc"].at[row, low:high], o.at[TAPS + n, 0 : high - low]),) * 2)
        waits = []
        for i, (one, other) in enumerate(jobs):
            one, other = (pltpu.make_async_copy(*c, sems.at[i]) for c in (one, other))
            pl.when(even)(one.start)
            pl.when(~even)(other.start)
            waits.append(one)
        for wait in waits:
            wait.wait()

    count = 2 * (len(depth) + len(arr_depth)) + 2 * (1 + extra)
    sources_in = {"enc": enc_in, "dec": dec_in, "skip": skip, "arr": arr, "e": e_own}
    pay = call(
        sources_in,
        [((starts[-1],) + image, BF)] * 2
        + [((arr_starts[-1],) + image, BF)] * 2
        + [((TAPS + extra, ke, outs), BF)] * 2,
        pack,
        [pltpu.SemaphoreType.DMA((count,))],
        where={n: "hbm" for n in sources_in},
    )

    def join(far):
        def body(ins, out, scratch):
            out[0][:ne] = ins["w"][...].reshape(ne, outs)
            out[0][ne:] = ins["rims"][...].reshape(-1, outs)

        return call({"w": far, "rims": pay[0]}, [((ne + starts[-1] * width, outs), BF)], body)[0]

    def pick(ins, out, scratch):
        even = lax.rem(lax.axis_index("rows"), 2) == 0
        copies = [pltpu.make_async_copy(ins[n], out[0], scratch[0]) for n in ("ahead", "behind")]
        pl.when(even)(copies[0].start)
        pl.when(~even)(copies[1].start)
        copies[0].wait()

    e_pieces = {"p0": pay[4], "p1": send(pay[4], ahead), "p2": send(pay[5], behind)}
    e_pieces["p3"] = send(e_own, across)
    e_pieces["p4"] = send(e_own, opposite)
    e_pieces["p5"] = send(e_pieces["p3"], ahead)
    e_pieces["p6"] = send(e_pieces["p3"], behind)
    e_pieces["p7"] = send(join(e_pieces["p4"]), across)

    d_pieces = {"p0": d_own, "p1": send(d_own, ahead), "p2": send(d_own, behind)}
    d_pieces["p3"] = send(d_own, across)
    picked = call(
        {"ahead": d_pieces["p1"], "behind": d_pieces["p2"]},
        [(d_own.shape, BF)],
        pick,
        [pltpu.SemaphoreType.DMA(())],
        where={"ahead": "any", "behind": "any"},
    )[0]
    forward = pairs(lambda s, r: (s, (r - 2) % ring if r % 2 else (r + 2) % ring))
    d_pieces["p4"] = send(picked, forward)
    d_pieces["p5"] = send(d_pieces["p3"], ahead)
    d_pieces["p6"] = send(d_pieces["p3"], behind)
    d_pieces["p7"] = send(d_pieces["p4"], across)
    rims = {"pair": e_pieces["p7"], "cross": send(pay[1], cross)}
    arr_rims = {"pair": send(pay[2], first_across), "cross": send(pay[3], first_cross)}

    def around(pair, cross_rim, middle, before=0, after=0, also=None):
        even = lax.rem(lax.axis_index("rows"), 2) == 0
        both = lambda c: c if also is None else c & also
        return [
            (both(even), [before, cross_rim, middle, pair, after]),
            (both(~even), [before, pair, middle, cross_rim, after]),
        ]

    def rim_rows(ins, n):
        low, high = starts[n], starts[n + 1]
        pair = ins["pair"] if "pair" in ins else ins["p7"]
        return pair.at[ne + low * width : ne + high * width], ins["cross"].at[low:high]

    def arr_rows(ins, t):
        return [ins[n].at[arr_starts[t] : arr_starts[t + 1]] for n in ("pair", "cross")]

    def begin(jobs, sems, at=0):
        copies = [pltpu.make_async_copy(*job, sems.at[at + i]) for i, job in enumerate(jobs)]
        for copy in copies:
            copy.start()
        return copies

    def moves(piece, k, w_ref, place):
        if len(piece.shape) == 3:
            return [(piece.at[0:TAPS], w_ref.at[:, place])]
        return [(piece.at[t * k : (t + 1) * k], w_ref.at[t, place]) for t in range(TAPS)]

    bias_scratch = [pltpu.VMEM((1, outs), F32), pltpu.SemaphoreType.DMA((1,))]

    def x_scratch(rows):
        return pltpu.VMEM((rows,) + image, BF)

    def y_scratch(rows):
        return pltpu.VMEM((3, rows * width, outs), F32)

    def cost(rows, groups=1):
        return 4 * rows * width * TAPS * groups * channels * outs

    def enc0_body(ins, out, scratch):
        x_ref, y_ref, sems, bias_ref, few = scratch
        w_ref = out[1]
        (bias,) = begin([(ins["bias"], bias_ref)], few)
        jobs = []
        for i, source in enumerate(sources(ring)):
            place = pl.ds(pl.multiple_of(source * ke, ke), ke)
            jobs += moves(ins[f"p{i}"], ke, w_ref, place)
        copies = begin(jobs, sems)
        for n, low, high in chunks:
            x_ref[0, low:high] = ins["p1"][TAPS + n, 0 : high - low]
            x_ref[own + 7, low:high] = ins["p2"][TAPS + n, 0 : high - low]
        fill(x_ref, around(*rim_rows(ins, 0), ins["enc"], 1, 1), own, total)
        for copy in copies:
            copy.wait()

        def store(row, v):
            out[0][row] = v

        finish([x_ref], [w_ref], y_ref, bias_ref, bias, None, store)

    e0, w_enc = call(
        {**e_pieces, "cross": rims["cross"], "enc": enc_in, "bias": encoder_bias},
        [((own + 6,) + image, BF), ((TAPS, ke * ring, outs), BF)],
        enc0_body,
        [x_scratch(own + 8), y_scratch(own + 6), pltpu.SemaphoreType.DMA((7 + TAPS,))]
        + bias_scratch,
        cost(own + 6),
        {"p3": "any", "p4": "any", "p5": "any", "p6": "any", "bias": "hbm"},
    )

    def enc_body(t, ins, out, scratch):
        x_ref, y_ref, bias_ref, few = scratch
        (bias,) = begin([(ins["bias"], bias_ref)], few)
        first = lax.axis_index("segment") == 0
        cases = [(~first, [ins["moved"]])]
        cases += around(*arr_rows(ins, t), ins["arr"].at[t], also=first)
        fill(x_ref, cases, own, total)
        if t < 2:

            def store(row, v):
                out[0][row] = v
        else:
            for n in range(3):
                out[0][n] = ins[f"e{n}"][3 - n : 3 - n + own]

            def store(row, v):
                out[0][3, row] = v

        finish([x_ref], [ins["w"]], y_ref, bias_ref, bias, None, store)

    made = [e0]
    for t in range(3):
        rows = own + 4 - 2 * t
        arrays = {"moved": send(made[t], up), **arr_rims, "arr": arr}
        arrays |= {"w": w_enc, "bias": encoder_bias}
        if t == 2:
            arrays |= {f"e{n}": made[n] for n in range(3)}
        shape = ((rows,) if t < 2 else (4, own)) + image
        made += call(
            arrays,
            [(shape, BF)],
            lambda ins, out, scratch, t=t: enc_body(t, ins, out, scratch),
            [x_scratch(rows + 2), y_scratch(rows)] + bias_scratch,
            cost(rows),
            {"bias": "hbm"},
        )
    enc_all = made.pop()

    def dec0_body(ins, out, scratch):
        x_ref, s_ref, y_ref, sems, bias_ref, few = scratch
        halves = out[1:3]
        (bias,) = begin([(ins["bias"], bias_ref)], few)
        half = ring // 2
        waits = []
        for i, source in enumerate(sources(ring)):
            place = pl.ds(pl.multiple_of(lax.rem(source, half) * kd, kd), kd)
            jobs = [moves(ins[f"p{i}"], kd, w, place)[0] for w in halves]
            copies = [pltpu.make_async_copy(*job, sems.at[i]) for job in jobs]
            pl.when(source < half)(copies[0].start)
            pl.when(source >= half)(copies[1].start)
            waits.append(copies[0])
        fill(x_ref, around(*rim_rows(ins, 1), ins["dec"]), own, total)
        fill(s_ref, around(*rim_rows(ins, 2), ins["skip"].at[0]), own, total)
        for copy in waits:
            copy.wait()

        def store(row, v):
            out[0][row] = v

        finish([x_ref, s_ref], halves, y_ref, bias_ref, bias, None, store)

    w_half = ((TAPS, kd * ring // 2, outs), BF)
    d0, w_dec, w_skip = call(
        {**d_pieces, **rims, "dec": dec_in, "skip": skip, "bias": decoder_bias},
        [((own + 2,) + image, BF), w_half, w_half],
        dec0_body,
        [x_scratch(own + 4)] * 2
        + [y_scratch(own + 2), pltpu.SemaphoreType.DMA((8,))]
        + bias_scratch,
        cost(own + 2, 2),
        {"bias": "hbm"} | {f"p{i}": "any" for i in range(8)},
    )

    handed = {1: ("e0", 2, own + 2), 2: ("e1", 0, own + 4), 3: ("e2", 0, own + 2)}
    results = {f"e{n}": made[n] for n in range(3)}

    def handed_view(ins, t):
        name, at, rows = handed[t]
        return ins[name].at[at : at + rows]

    skip_rows = [own, own + 2, own]

    def skip_body(ins, out, scratch):
        x_refs, y_ref = scratch[:3], scratch[3]
        lag = 2 * (segments - lax.axis_index("segment")) - 1
        for t in range(1, 4):
            cases = [(lag == 1, [handed_view(ins, t)])]
            plain = lag != 1
            if t == 3:
                cases.append((lag == 3, [handed_view(ins, 1)]))
                plain = plain & (lag != 3)
            cases += around(*rim_rows(ins, 2 + t), ins["skip"].at[t], also=plain)
            fill(x_refs[t - 1], cases, own, total)
        left = jnp.concatenate([patches(x) for x in x_refs], axis=0)
        products(left, [ins["w"]], y_ref)
        at = 0
        for o in out:
            for row in range(o.shape[0]):
                o[row] = combine(y_ref, at, width)
                at += 1

    acc = call(
        {**rims, **results, "skip": skip, "w": w_skip},
        [((r,) + image[:1] + (outs,), F32) for r in skip_rows],
        skip_body,
        [x_scratch(r + 2) for r in skip_rows] + [y_scratch(sum(skip_rows))],
        cost(sum(skip_rows)),
    )

    def dec_body(t, moved, ins, out, scratch):
        x_ref, y_ref, bias_ref, few = scratch
        (bias,) = begin([(ins["bias"], bias_ref)], few)
        last = lax.axis_index("segment") == segments - 1
        cases = [(~last, [ins[m] for m in moved]), (last, [handed_view(ins, t)])]
        fill(x_ref, cases, own, total)
        if t == 3:
            out[0][0] = ins["d0"][1 : 1 + own]
            out[0][1] = ins["d1"][...]
            out[0][2] = ins["d2"][1 : 1 + own]

        def store(row, v):
            if t == 3:
                out[0][3, row] = v
            else:
                out[0][row] = v
            if t == 1 and row < 2:
                out[1][row] = v
            if t == 1 and row >= own - 2:
                out[2][row - own + 2] = v

        finish([x_ref], [ins["w"]], y_ref, bias_ref, bias, ins["acc"], store)

    def dec(t, rows, moved, shapes, more=()):
        arrays = dict(moved)
        name = handed[t][0]
        arrays |= {name: results[name], "w": w_dec, "bias": decoder_bias, "acc": acc[t - 1]}
        arrays |= dict(more)
        return call(
            arrays,
            [(s + image, BF) for s in shapes],
            lambda ins, out, scratch: dec_body(t, list(moved), ins, out, scratch),
            [x_scratch(rows + 2), y_scratch(rows)] + bias_scratch,
            cost(rows),
            {"bias": "hbm"},
        )

    d1, d1_head, d1_last = dec(1, own, {"m": send(d0, down)}, [(own,), (2,), (2,)])
    moved = {
        "before": send(d1_last, down_after),
        "m": send(d1, down),
        "after": send(d1_head, down_before),
    }
    (d2,) = dec(2, own + 2, moved, [(own + 2,)])
    (dec_all,) = dec(3, own, {"m": send(d2, down)}, [(4, own)], {"d0": d0, "d1": d1, "d2": d2})
    shape = (1, 4, 1, own, width, outs)
    return enc_all.reshape(shape), dec_all.reshape(shape)


def solution(mesh):
    return jax.shard_map(
        shards,
        mesh=mesh,
        in_specs=(
            P("segment", None, None, "rows", None),
            P("segment", None),
            P("segment", None, None, "rows", None),
            P("segment", None),
            P("segment", None, "rows", None, None),
            P("segment", None, "rows", None, None),
            P(None, None, "rows", None, None),
            P("segment", None, None, "rows", None, None),
        ),
        out_specs=(
            P("segment", None, None, "rows", None, None),
            P("segment", None, None, "rows", None, None),
        ),
        check_vma=False,
    )
```

profile of v0, /device:TPU:377, one launch (start us, length us, event | category | flops | bytes accessed | tf_op | source)
XLA Modules:
  0.0 151.4 jit_solution(726947350027242806)
XLA Ops:
  0.6 4.5 %collective-permute-start.14 = (bf16[9,96,384]{2,1,0:T(8,128)(2,1)}, bf16[9,96,384]{2,1,0:T(8,128)(2,1)S(1)}, u32[]{:S(2)}, u32[]{:S(2)}) collective-permute-start(bf16[9,96,384]{2,1,0:T(8,128)(2,1)} %bitcast.23), channel_id=1, source_target_pairs={{0,6},{1,7},{2,0},{3,1},{4,2},{5,3},{6,4},{7,5},{8,14},{9,15},{10,... | collective-permute-start | bytes 1990664 | tf_op jit(solution)/shard_map/ppermute | solution.py:149
  5.2 2.4 %collective-permute-start.3 = (bf16[9,48,384]{2,1,0:T(8,128)(2,1)}, bf16[9,48,384]{2,1,0:T(8,128)(2,1)S(1)}, u32[]{:S(2)}, u32[]{:S(2)}) collective-permute-start(bf16[9,48,384]{2,1,0:T(8,128)(2,1)} %bitcast.29), channel_id=1, source_target_pairs={{0,4},{1,5},{2,6},{3,7},{4,0},{5,1},{6,2},{7,3},{8,12},{9,13},{10,... | collective-permute-start | bytes 995336 | tf_op jit(solution)/shard_map/ppermute | solution.py:149
  7.6 2.9 %collective-permute-start.2 = (bf16[9,48,384]{2,1,0:T(8,128)(2,1)}, bf16[9,48,384]{2,1,0:T(8,128)(2,1)S(1)}, u32[]{:S(2)}, u32[]{:S(2)}) collective-permute-start(bf16[9,48,384]{2,1,0:T(8,128)(2,1)} %bitcast.30), channel_id=1, source_target_pairs={{0,1},{1,0},{2,3},{3,2},{4,5},{5,4},{6,7},{7,6},{8,9},{9,8},{10,11... | collective-permute-start | bytes 995336 | tf_op jit(solution)/shard_map/ppermute | solution.py:149
  10.5 2.5 %collective-permute-start.13 = (bf16[9,96,384]{2,1,0:T(8,128)(2,1)}, bf16[9,96,384]{2,1,0:T(8,128)(2,1)S(1)}, u32[]{:S(2)}, u32[]{:S(2)}) collective-permute-start(bf16[9,96,384]{2,1,0:T(8,128)(2,1)} %bitcast.24), channel_id=1, source_target_pairs={{0,2},{1,3},{2,4},{3,5},{4,6},{5,7},{6,0},{7,1},{8,10},{9,11},{10,... | collective-permute-start | bytes 1990664 | tf_op jit(solution)/shard_map/ppermute | solution.py:149
  15.0 5.1 %collective-permute-start.7 = (bf16[11,64,384]{2,1,0:T(8,128)(2,1)S(1)}, bf16[11,64,384]{2,1,0:T(8,128)(2,1)S(1)}, u32[]{:S(2)}, u32[]{:S(2)}) collective-permute-start(bf16[11,64,384]{2,1,0:T(8,128)(2,1)S(1)} %get-tuple-element.22), channel_id=1, source_target_pairs={{1,2},{2,1},{3,4},{4,3},{5,6},{6,5},{9,10},{10,9},{11,12},{12,11},... | collective-permute-start | bytes 1622024 | tf_op jit(solution)/shard_map/ppermute | solution.py:149
  22.2 10.9 %collective-permute-start.1 = (bf16[11,48,384]{2,1,0:T(8,128)(2,1)S(1)}, bf16[11,48,384]{2,1,0:T(8,128)(2,1)S(1)}, u32[]{:S(2)}, u32[]{:S(2)}) collective-permute-start(bf16[11,48,384]{2,1,0:T(8,128)(2,1)S(1)} %get-tuple-element.20), channel_id=1, source_target_pairs={{0,6},{1,7},{2,0},{3,1},{4,2},{5,3},{6,4},{7,5},{8,14},{9,15},{10,... | collective-permute-start | bytes 1216520 | tf_op jit(solution)/shard_map/ppermute | solution.py:149
  35.1 3.9 %collective-permute-start.15 = (bf16[9,96,384]{2,1,0:T(8,128)(2,1)S(1)}, bf16[9,96,384]{2,1,0:T(8,128)(2,1)S(1)}, u32[]{:S(2)}, u32[]{:S(2)}) collective-permute-start(bf16[9,96,384]{2,1,0:T(8,128)(2,1)S(1)} %bitcast.25), channel_id=1, source_target_pairs={{0,1},{1,0},{2,3},{3,2},{4,5},{5,4},{6,7},{7,6},{8,9},{9,8},{10,11... | collective-permute-start | bytes 1990664 | tf_op jit(solution)/shard_map/ppermute | solution.py:149
  39.6 4.5 %collective-permute-start.16 = (bf16[9,96,384]{2,1,0:T(8,128)(2,1)S(1)}, bf16[9,96,384]{2,1,0:T(8,128)(2,1)S(1)}, u32[]{:S(2)}, u32[]{:S(2)}) collective-permute-start(bf16[9,96,384]{2,1,0:T(8,128)(2,1)S(1)} %shard_map.101), channel_id=1, source_target_pairs={{0,2},{1,7},{2,4},{3,1},{4,6},{5,3},{6,0},{7,5},{8,10},{9,15},{10,... | collective-permute-start | bytes 1990664 | tf_op jit(solution)/shard_map/ppermute | solution.py:149
  44.2 4.4 %collective-permute-done.refs_1_ = bf16[11,48,384]{2,1,0:T(8,128)(2,1)S(1)} collective-permute-done((bf16[11,48,384]{2,1,0:T(8,128)(2,1)S(1)}, bf16[11,48,384]{2,1,0:T(8,128)(2,1)S(1)}, u32[]{:S(2)}, u32[]{:S(2)}) %collective-permute-start) | collective-permute-done | bytes 405536 | tf_op jit(solution)/shard_map/ppermute | solution.py:149
  48.5 5.4 %collective-permute-start.5 = (bf16[9,48,384]{2,1,0:T(8,128)(2,1)S(1)}, bf16[9,48,384]{2,1,0:T(8,128)(2,1)S(1)}, u32[]{:S(2)}, u32[]{:S(2)}) collective-permute-start(bf16[9,48,384]{2,1,0:T(8,128)(2,1)S(1)} %collective-permute-done.2.refs_3_), channel_id=1, source_target_pairs={{0,6},{1,7},{2,0},{3,1},{4,2},{5,3},{6,4},{7,5},{8,14},{9,15},{10,... | collective-permute-start | bytes 995336 | tf_op jit(solution)/shard_map/ppermute | solution.py:149
  55.8 5.9 %collective-permute-done.5.refs_6_ = bf16[9,48,384]{2,1,0:T(8,128)(2,1)S(1)} collective-permute-done((bf16[9,48,384]{2,1,0:T(8,128)(2,1)S(1)}, bf16[9,48,384]{2,1,0:T(8,128)(2,1)S(1)}, u32[]{:S(2)}, u32[]{:S(2)}) %collective-permute-start.5) | collective-permute-done | bytes 331808 | tf_op jit(solution)/shard_map/ppermute | solution.py:149
  64.3 3.8 %shard_map.97 = (bf16[9,64,384]{2,1,0:T(8,128)(2,1)S(1)}, bf16[9,384,384]{2,1,0:T(8,128)(2,1)S(1)}) custom-call(bf16[11,48,384]{2,1,0:T(8,128)(2,1)S(1)} %get-tuple-element.19.refs_0_, bf16[11,48,384]{2,1,0:T(8,128)(2,1)S(1)} %collective-permute-done.refs_1_, bf16[11,48,384]{2,1,0:T(8,128)(2,1)S(1)} %collective-permute-done.1.refs_2_, ...), custom_call_target="tpu_custom_call" | custom-call | flops 3057647616 | bytes 4105728 | tf_op jit(solution)/shard_map/pallas_call | solution.py:32
  68.1 5.7 %collective-permute-start.8 = (bf16[9,64,384]{2,1,0:T(8,128)(2,1)S(1)}, bf16[9,64,384]{2,1,0:T(8,128)(2,1)S(1)}, u32[]{:S(2)}, u32[]{:S(2)}) collective-permute-start(bf16[9,64,384]{2,1,0:T(8,128)(2,1)S(1)} %get-tuple-element.23.refs_6_.refs_2_.refs_1_), channel_id=1, source_target_pairs={{0,8},{1,9},{2,10},{3,11},{4,12},{5,13},{6,14},{7,15},{8,16},{9,17... | collective-permute-start | bytes 1327112 | tf_op jit(solution)/shard_map/ppermute | solution.py:149
  73.8 5.0 %collective-permute-start.18 = (bf16[9,96,384]{2,1,0:T(8,128)(2,1)S(1)}, bf16[9,96,384]{2,1,0:T(8,128)(2,1)S(1)}, u32[]{:S(2)}, u32[]{:S(2)}) collective-permute-start(bf16[9,96,384]{2,1,0:T(8,128)(2,1)S(1)} %collective-permute-done.15.refs_3_), channel_id=1, source_target_pairs={{0,6},{1,7},{2,0},{3,1},{4,2},{5,3},{6,4},{7,5},{8,14},{9,15},{10,... | collective-permute-start | bytes 1990664 | tf_op jit(solution)/shard_map/ppermute | solution.py:149
  80.7 7.6 %collective-permute-start.19 = (bf16[9,96,384]{2,1,0:T(8,128)(2,1)S(1)}, bf16[9,96,384]{2,1,0:T(8,128)(2,1)S(1)}, u32[]{:S(2)}, u32[]{:S(2)}) collective-permute-start(bf16[9,96,384]{2,1,0:T(8,128)(2,1)S(1)} %collective-permute-done.16.refs_4_), channel_id=1, source_target_pairs={{0,1},{1,0},{2,3},{3,2},{4,5},{5,4},{6,7},{7,6},{8,9},{9,8},{10,11... | collective-permute-start | bytes 1990664 | tf_op jit(solution)/shard_map/ppermute | solution.py:149
  93.4 5.0 %collective-permute-done.17.refs_5_ = bf16[9,96,384]{2,1,0:T(8,128)(2,1)S(1)} collective-permute-done((bf16[9,96,384]{2,1,0:T(8,128)(2,1)S(1)}, bf16[9,96,384]{2,1,0:T(8,128)(2,1)S(1)}, u32[]{:S(2)}, u32[]{:S(2)}) %collective-permute-start.17) | collective-permute-done | bytes 663584 | tf_op jit(solution)/shard_map/ppermute | solution.py:149
  98.5 9.0 %collective-permute-done.19.refs_7_ = bf16[9,96,384]{2,1,0:T(8,128)(2,1)S(1)} collective-permute-done((bf16[9,96,384]{2,1,0:T(8,128)(2,1)S(1)}, bf16[9,96,384]{2,1,0:T(8,128)(2,1)S(1)}, u32[]{:S(2)}, u32[]{:S(2)}) %collective-permute-start.19) | collective-permute-done | bytes 663584 | tf_op jit(solution)/shard_map/ppermute | solution.py:149
  107.4 3.4 %shard_map.102 = (bf16[5,64,384]{2,1,0:T(8,128)(2,1)S(1)}, bf16[9,384,384]{2,1,0:T(8,128)(2,1)S(1)}, bf16[9,384,384]{2,1,0:T(8,128)(2,1)S(1)}) custom-call(bf16[9,96,384]{2,1,0:T(8,128)(2,1)S(1)} %bitcast.26, bf16[9,96,384]{2,1,0:T(8,128)(2,1)S(1)} %collective-permute-done.13.refs_0_.refs_1_, ...), custom_call_target="tpu_custom_call" | custom-call | flops 3397386240 | bytes 7460352 | tf_op jit(solution)/shard_map/pallas_call | solution.py:32
  114.9 3.2 %shard_map.103 = (f32[3,64,384]{2,1,0:T(8,128)S(1)}, f32[5,64,384]{2,1,0:T(8,128)S(1)}, f32[3,64,384]{2,1,0:T(8,128)S(1)}) custom-call(bf16[1136,384]{1,0:T(8,128)(2,1)S(1)} %collective-permute-done.6.refs_7_.refs_8_.refs_0_, bf16[11,64,384]{2,1,0:T(8,128)(2,1)S(1)} %collective-permute-done.7.refs_8_.refs_9_.refs_1_, ...), custom_call_target="tpu_custom_call" | custom-call | flops 3737124864 | bytes 5689344 | tf_op jit(solution)/shard_map/pallas_call | solution.py:32
  118.1 2.4 %collective-permute-done.20.refs_0_ = bf16[5,64,384]{2,1,0:T(8,128)(2,1)S(1)} collective-permute-done((bf16[5,64,384]{2,1,0:T(8,128)(2,1)S(1)}, bf16[5,64,384]{2,1,0:T(8,128)(2,1)S(1)}, u32[]{:S(2)}, u32[]{:S(2)}) %collective-permute-start.20) | collective-permute-done | bytes 245792 | tf_op jit(solution)/shard_map/ppermute | solution.py:149
  123.5 4.2 %collective-permute-start.21 = (bf16[2,64,384]{2,1,0:T(8,128)(2,1)S(1)}, bf16[2,64,384]{2,1,0:T(8,128)(2,1)S(1)}, u32[]{:S(2)}, u32[]{:S(2)}) collective-permute-start(bf16[2,64,384]{2,1,0:T(8,128)(2,1)S(1)} %get-tuple-element.31), channel_id=1, source_target_pairs={{8,1},{9,2},{10,3},{11,4},{12,5},{13,6},{14,7},{16,9},{17,10},{18,... | collective-permute-start | bytes 294920 | tf_op jit(solution)/shard_map/ppermute | solution.py:149
  129.7 5.3 %collective-permute-start.12 = (bf16[5,64,384]{2,1,0:T(8,128)(2,1)S(1)}, bf16[5,64,384]{2,1,0:T(8,128)(2,1)S(1)}, u32[]{:S(2)}, u32[]{:S(2)}) collective-permute-start(bf16[5,64,384]{2,1,0:T(8,128)(2,1)S(1)} %shard_map.99.refs_8_.refs_4_.refs_1_), channel_id=1, source_target_pairs={{0,8},{1,9},{2,10},{3,11},{4,12},{5,13},{6,14},{7,15},{8,16},{9,17... | collective-permute-start | bytes 737288 | tf_op jit(solution)/shard_map/ppermute | solution.py:149
  135.0 2.9 %collective-permute-done.23.refs_2_ = bf16[2,64,384]{2,1,0:T(8,128)(2,1)S(1)} collective-permute-done((bf16[2,64,384]{2,1,0:T(8,128)(2,1)S(1)}, bf16[2,64,384]{2,1,0:T(8,128)(2,1)S(1)}, u32[]{:S(2)}, u32[]{:S(2)}) %collective-permute-start.23) | collective-permute-done | bytes 98336 | tf_op jit(solution)/shard_map/ppermute | solution.py:149
  143.6 5.7 %collective-permute-done.24.refs_0_ = bf16[5,64,384]{2,1,0:T(8,128)(2,1)S(1)} collective-permute-done((bf16[5,64,384]{2,1,0:T(8,128)(2,1)S(1)}, bf16[5,64,384]{2,1,0:T(8,128)(2,1)S(1)}, u32[]{:S(2)}, u32[]{:S(2)}) %collective-permute-start.24) | collective-permute-done | bytes 245792 | tf_op jit(solution)/shard_map/ppermute | solution.py:149
  (48 shorter events, 34.6 us)
Async XLA Ops:
  0.6 32.5 %collective-permute-start.14 = (bf16[9,96,384]{2,1,0:T(8,128)(2,1)}, bf16[9,96,384]{2,1,0:T(8,128)(2,1)S(1)}, u32[]{:S(2)}, u32[]{:S(2)}) collective-permute-start(bf16[9,96,384]{2,1,0:T(8,128)(2,1)} %bitcast.23), channel_id=1, source_target_pairs={{0,6},{1,7},{2,0},{3,1},{4,2},{5,3},{6,4},{7,5},{8,14},{9,15},{10,... | collective-permute-start | bytes 1990664 | tf_op jit(solution)/shard_map/ppermute | solution.py:149
  5.2 15.0 %collective-permute-start.3 = (bf16[9,48,384]{2,1,0:T(8,128)(2,1)}, bf16[9,48,384]{2,1,0:T(8,128)(2,1)S(1)}, u32[]{:S(2)}, u32[]{:S(2)}) collective-permute-start(bf16[9,48,384]{2,1,0:T(8,128)(2,1)} %bitcast.29), channel_id=1, source_target_pairs={{0,4},{1,5},{2,6},{3,7},{4,0},{5,1},{6,2},{7,3},{8,12},{9,13},{10,... | collective-permute-start | bytes 995336 | tf_op jit(solution)/shard_map/ppermute | solution.py:149
  7.6 14.6 %collective-permute-start.2 = (bf16[9,48,384]{2,1,0:T(8,128)(2,1)}, bf16[9,48,384]{2,1,0:T(8,128)(2,1)S(1)}, u32[]{:S(2)}, u32[]{:S(2)}) collective-permute-start(bf16[9,48,384]{2,1,0:T(8,128)(2,1)} %bitcast.30), channel_id=1, source_target_pairs={{0,1},{1,0},{2,3},{3,2},{4,5},{5,4},{6,7},{7,6},{8,9},{9,8},{10,11... | collective-permute-start | bytes 995336 | tf_op jit(solution)/shard_map/ppermute | solution.py:149
  10.5 24.6 %collective-permute-start.13 = (bf16[9,96,384]{2,1,0:T(8,128)(2,1)}, bf16[9,96,384]{2,1,0:T(8,128)(2,1)S(1)}, u32[]{:S(2)}, u32[]{:S(2)}) collective-permute-start(bf16[9,96,384]{2,1,0:T(8,128)(2,1)} %bitcast.24), channel_id=1, source_target_pairs={{0,2},{1,3},{2,4},{3,5},{4,6},{5,7},{6,0},{7,1},{8,10},{9,11},{10,... | collective-permute-start | bytes 1990664 | tf_op jit(solution)/shard_map/ppermute | solution.py:149
  15.0 38.9 %collective-permute-start.7 = (bf16[11,64,384]{2,1,0:T(8,128)(2,1)S(1)}, bf16[11,64,384]{2,1,0:T(8,128)(2,1)S(1)}, u32[]{:S(2)}, u32[]{:S(2)}) collective-permute-start(bf16[11,64,384]{2,1,0:T(8,128)(2,1)S(1)} %get-tuple-element.22), channel_id=1, source_target_pairs={{1,2},{2,1},{3,4},{4,3},{5,6},{6,5},{9,10},{10,9},{11,12},{12,11},... | collective-permute-start | bytes 1622024 | tf_op jit(solution)/shard_map/ppermute | solution.py:149
  20.2 44.1 %collective-permute-start.6 = (bf16[1136,384]{1,0:T(8,128)(2,1)S(1)}, bf16[1136,384]{1,0:T(8,128)(2,1)S(1)}, u32[]{:S(2)}, u32[]{:S(2)}) collective-permute-start(bf16[1136,384]{1,0:T(8,128)(2,1)S(1)} %shard_map.96), channel_id=1, source_target_pairs={{0,1},{1,0},{2,3},{3,2},{4,5},{5,4},{6,7},{7,6},{8,9},{9,8},{10,11... | collective-permute-start | bytes 2617352 | tf_op jit(solution)/shard_map/ppermute | solution.py:149
  22.2 17.5 %collective-permute-start.1 = (bf16[11,48,384]{2,1,0:T(8,128)(2,1)S(1)}, bf16[11,48,384]{2,1,0:T(8,128)(2,1)S(1)}, u32[]{:S(2)}, u32[]{:S(2)}) collective-permute-start(bf16[11,48,384]{2,1,0:T(8,128)(2,1)S(1)} %get-tuple-element.20), channel_id=1, source_target_pairs={{0,6},{1,7},{2,0},{3,1},{4,2},{5,3},{6,4},{7,5},{8,14},{9,15},{10,... | collective-permute-start | bytes 1216520 | tf_op jit(solution)/shard_map/ppermute | solution.py:149
  33.1 15.4 %collective-permute-start = (bf16[11,48,384]{2,1,0:T(8,128)(2,1)S(1)}, bf16[11,48,384]{2,1,0:T(8,128)(2,1)S(1)}, u32[]{:S(2)}, u32[]{:S(2)}) collective-permute-start(bf16[11,48,384]{2,1,0:T(8,128)(2,1)S(1)} %get-tuple-element.19.refs_0_), channel_id=1, source_target_pairs={{0,2},{1,3},{2,4},{3,5},{4,6},{5,7},{6,0},{7,1},{8,10},{9,11},{10,... | collective-permute-start | bytes 1216520 | tf_op jit(solution)/shard_map/ppermute | solution.py:149
  35.1 38.7 %collective-permute-start.15 = (bf16[9,96,384]{2,1,0:T(8,128)(2,1)S(1)}, bf16[9,96,384]{2,1,0:T(8,128)(2,1)S(1)}, u32[]{:S(2)}, u32[]{:S(2)}) collective-permute-start(bf16[9,96,384]{2,1,0:T(8,128)(2,1)S(1)} %bitcast.25), channel_id=1, source_target_pairs={{0,1},{1,0},{2,3},{3,2},{4,5},{5,4},{6,7},{7,6},{8,9},{9,8},{10,11... | collective-permute-start | bytes 1990664 | tf_op jit(solution)/shard_map/ppermute | solution.py:149
  39.6 41.0 %collective-permute-start.16 = (bf16[9,96,384]{2,1,0:T(8,128)(2,1)S(1)}, bf16[9,96,384]{2,1,0:T(8,128)(2,1)S(1)}, u32[]{:S(2)}, u32[]{:S(2)}) collective-permute-start(bf16[9,96,384]{2,1,0:T(8,128)(2,1)S(1)} %shard_map.101), channel_id=1, source_target_pairs={{0,2},{1,7},{2,4},{3,1},{4,6},{5,3},{6,0},{7,5},{8,10},{9,15},{10,... | collective-permute-start | bytes 1990664 | tf_op jit(solution)/shard_map/ppermute | solution.py:149
  48.5 13.2 %collective-permute-start.5 = (bf16[9,48,384]{2,1,0:T(8,128)(2,1)S(1)}, bf16[9,48,384]{2,1,0:T(8,128)(2,1)S(1)}, u32[]{:S(2)}, u32[]{:S(2)}) collective-permute-start(bf16[9,48,384]{2,1,0:T(8,128)(2,1)S(1)} %collective-permute-done.2.refs_3_), channel_id=1, source_target_pairs={{0,6},{1,7},{2,0},{3,1},{4,2},{5,3},{6,4},{7,5},{8,14},{9,15},{10,... | collective-permute-start | bytes 995336 | tf_op jit(solution)/shard_map/ppermute | solution.py:149
  53.9 10.4 %collective-permute-start.4 = (bf16[9,48,384]{2,1,0:T(8,128)(2,1)S(1)}, bf16[9,48,384]{2,1,0:T(8,128)(2,1)S(1)}, u32[]{:S(2)}, u32[]{:S(2)}) collective-permute-start(bf16[9,48,384]{2,1,0:T(8,128)(2,1)S(1)} %collective-permute-done.2.refs_3_), channel_id=1, source_target_pairs={{0,2},{1,3},{2,4},{3,5},{4,6},{5,7},{6,0},{7,1},{8,10},{9,11},{10,... | collective-permute-start | bytes 995336 | tf_op jit(solution)/shard_map/ppermute | solution.py:149
  61.7 26.6 %collective-permute-start.9 = (bf16[6,64,384]{2,1,0:T(8,128)(2,1)S(1)}, bf16[6,64,384]{2,1,0:T(8,128)(2,1)S(1)}, u32[]{:S(2)}, u32[]{:S(2)}) collective-permute-start(bf16[6,64,384]{2,1,0:T(8,128)(2,1)S(1)} %get-tuple-element.24), channel_id=1, source_target_pairs={{0,1},{1,0},{2,3},{3,2},{4,5},{5,4},{6,7},{7,6}} | collective-permute-start | bytes 884744 | tf_op jit(solution)/shard_map/ppermute | solution.py:149
  68.1 21.0 %collective-permute-start.8 = (bf16[9,64,384]{2,1,0:T(8,128)(2,1)S(1)}, bf16[9,64,384]{2,1,0:T(8,128)(2,1)S(1)}, u32[]{:S(2)}, u32[]{:S(2)}) collective-permute-start(bf16[9,64,384]{2,1,0:T(8,128)(2,1)S(1)} %get-tuple-element.23.refs_6_.refs_2_.refs_1_), channel_id=1, source_target_pairs={{0,8},{1,9},{2,10},{3,11},{4,12},{5,13},{6,14},{7,15},{8,16},{9,17... | collective-permute-start | bytes 1327112 | tf_op jit(solution)/shard_map/ppermute | solution.py:149
  73.8 19.7 %collective-permute-start.18 = (bf16[9,96,384]{2,1,0:T(8,128)(2,1)S(1)}, bf16[9,96,384]{2,1,0:T(8,128)(2,1)S(1)}, u32[]{:S(2)}, u32[]{:S(2)}) collective-permute-start(bf16[9,96,384]{2,1,0:T(8,128)(2,1)S(1)} %collective-permute-done.15.refs_3_), channel_id=1, source_target_pairs={{0,6},{1,7},{2,0},{3,1},{4,2},{5,3},{6,4},{7,5},{8,14},{9,15},{10,... | collective-permute-start | bytes 1990664 | tf_op jit(solution)/shard_map/ppermute | solution.py:149
  78.7 19.7 %collective-permute-start.17 = (bf16[9,96,384]{2,1,0:T(8,128)(2,1)S(1)}, bf16[9,96,384]{2,1,0:T(8,128)(2,1)S(1)}, u32[]{:S(2)}, u32[]{:S(2)}) collective-permute-start(bf16[9,96,384]{2,1,0:T(8,128)(2,1)S(1)} %collective-permute-done.15.refs_3_), channel_id=1, source_target_pairs={{0,2},{1,3},{2,4},{3,5},{4,6},{5,7},{6,0},{7,1},{8,10},{9,11},{10,... | collective-permute-start | bytes 1990664 | tf_op jit(solution)/shard_map/ppermute | solution.py:149
  80.7 26.8 %collective-permute-start.19 = (bf16[9,96,384]{2,1,0:T(8,128)(2,1)S(1)}, bf16[9,96,384]{2,1,0:T(8,128)(2,1)S(1)}, u32[]{:S(2)}, u32[]{:S(2)}) collective-permute-start(bf16[9,96,384]{2,1,0:T(8,128)(2,1)S(1)} %collective-permute-done.16.refs_4_), channel_id=1, source_target_pairs={{0,1},{1,0},{2,3},{3,2},{4,5},{5,4},{6,7},{7,6},{8,9},{9,8},{10,11... | collective-permute-start | bytes 1990664 | tf_op jit(solution)/shard_map/ppermute | solution.py:149
  91.4 21.8 %collective-permute-start.11 = (bf16[7,64,384]{2,1,0:T(8,128)(2,1)S(1)}, bf16[7,64,384]{2,1,0:T(8,128)(2,1)S(1)}, u32[]{:S(2)}, u32[]{:S(2)}) collective-permute-start(bf16[7,64,384]{2,1,0:T(8,128)(2,1)S(1)} %shard_map.98.refs_7_.refs_3_), channel_id=1, source_target_pairs={{0,8},{1,9},{2,10},{3,11},{4,12},{5,13},{6,14},{7,15},{8,16},{9,17... | collective-permute-start | bytes 1032200 | tf_op jit(solution)/shard_map/ppermute | solution.py:149
  110.9 9.6 %collective-permute-start.20 = (bf16[5,64,384]{2,1,0:T(8,128)(2,1)S(1)}, bf16[5,64,384]{2,1,0:T(8,128)(2,1)S(1)}, u32[]{:S(2)}, u32[]{:S(2)}) collective-permute-start(bf16[5,64,384]{2,1,0:T(8,128)(2,1)S(1)} %get-tuple-element.27.refs_5_), channel_id=1, source_target_pairs={{8,0},{9,1},{10,2},{11,3},{12,4},{13,5},{14,6},{15,7},{16,8},{17,9... | collective-permute-start | bytes 737288 | tf_op jit(solution)/shard_map/ppermute | solution.py:149
  121.6 16.3 %collective-permute-start.22 = (bf16[3,64,384]{2,1,0:T(8,128)(2,1)S(1)}, bf16[3,64,384]{2,1,0:T(8,128)(2,1)S(1)}, u32[]{:S(2)}, u32[]{:S(2)}) collective-permute-start(bf16[3,64,384]{2,1,0:T(8,128)(2,1)S(1)} %get-tuple-element.32.refs_6_), channel_id=1, source_target_pairs={{8,0},{9,1},{10,2},{11,3},{12,4},{13,5},{14,6},{15,7},{16,8},{17,9... | collective-permute-start | bytes 442376 | tf_op jit(solution)/shard_map/ppermute | solution.py:149
  123.5 11.4 %collective-permute-start.21 = (bf16[2,64,384]{2,1,0:T(8,128)(2,1)S(1)}, bf16[2,64,384]{2,1,0:T(8,128)(2,1)S(1)}, u32[]{:S(2)}, u32[]{:S(2)}) collective-permute-start(bf16[2,64,384]{2,1,0:T(8,128)(2,1)S(1)} %get-tuple-element.31), channel_id=1, source_target_pairs={{8,1},{9,2},{10,3},{11,4},{12,5},{13,6},{14,7},{16,9},{17,10},{18,... | collective-permute-start | bytes 294920 | tf_op jit(solution)/shard_map/ppermute | solution.py:149
  127.8 10.2 %collective-permute-start.23 = (bf16[2,64,384]{2,1,0:T(8,128)(2,1)S(1)}, bf16[2,64,384]{2,1,0:T(8,128)(2,1)S(1)}, u32[]{:S(2)}, u32[]{:S(2)}) collective-permute-start(bf16[2,64,384]{2,1,0:T(8,128)(2,1)S(1)} %get-tuple-element.33), channel_id=1, source_target_pairs={{9,0},{10,1},{11,2},{12,3},{13,4},{14,5},{15,6},{17,8},{18,9},{19,... | collective-permute-start | bytes 294920 | tf_op jit(solution)/shard_map/ppermute | solution.py:149
  129.7 11.9 %collective-permute-start.12 = (bf16[5,64,384]{2,1,0:T(8,128)(2,1)S(1)}, bf16[5,64,384]{2,1,0:T(8,128)(2,1)S(1)}, u32[]{:S(2)}, u32[]{:S(2)}) collective-permute-start(bf16[5,64,384]{2,1,0:T(8,128)(2,1)S(1)} %shard_map.99.refs_8_.refs_4_.refs_1_), channel_id=1, source_target_pairs={{0,8},{1,9},{2,10},{3,11},{4,12},{5,13},{6,14},{7,15},{8,16},{9,17... | collective-permute-start | bytes 737288 | tf_op jit(solution)/shard_map/ppermute | solution.py:149
  139.7 9.6 %collective-permute-start.24 = (bf16[5,64,384]{2,1,0:T(8,128)(2,1)S(1)}, bf16[5,64,384]{2,1,0:T(8,128)(2,1)S(1)}, u32[]{:S(2)}, u32[]{:S(2)}) collective-permute-start(bf16[5,64,384]{2,1,0:T(8,128)(2,1)S(1)} %shard_map.105.refs_7_), channel_id=1, source_target_pairs={{8,0},{9,1},{10,2},{11,3},{12,4},{13,5},{14,6},{15,7},{16,8},{17,9... | collective-permute-start | bytes 737288 | tf_op jit(solution)/shard_map/ppermute | solution.py:149
  (6 other events, 150.5 us)
where the time goes:
time: 152 us; the launch traced here: 151 us
  starting transfers between devices  89.1 us (59%)
  waiting for transfers between devices  37.6 us (25%)
  Pallas kernels  23.4 us (15%)
    ppermute x25, starting transfers between devices, send(): return lax.ppermute(value, AXES, route)  89.1 us
    ppermute x25, waiting for transfers between devices, send(): return lax.ppermute(value, AXES, route)  37.6 us
    pallas_call x12, Pallas kernels, call(): pl.pallas_call(kernel, out_shape=shapes, in_specs=[pl.BlockSpec(memory_sp...  23.4 us
  transfers between devices with their start and end apart: 25, of which 10 were waited for; matrix products, arithmetic and copies ran while one was open for 0% of the time, Pallas kernels for 13%

commit v1 on v0

--- a/solution.py
+++ b/solution.py
@@ -400,34 +400,30 @@
         name, at, rows = handed[t]
         return ins[name].at[at : at + rows]
 
-    skip_rows = [own, own + 2, own]
-
-    def skip_body(ins, out, scratch):
-        x_refs, y_ref = scratch[:3], scratch[3]
+    def skip_body(t, ins, out, scratch):
+        x_ref, y_ref = scratch
         lag = 2 * (segments - lax.axis_index("segment")) - 1
-        for t in range(1, 4):
-            cases = [(lag == 1, [handed_view(ins, t)])]
-            plain = lag != 1
-            if t == 3:
-                cases.append((lag == 3, [handed_view(ins, 1)]))
-                plain = plain & (lag != 3)
-            cases += around(*rim_rows(ins, 2 + t), ins["skip"].at[t], also=plain)
-            fill(x_refs[t - 1], cases, own, total)
-        left = jnp.concatenate([patches(x) for x in x_refs], axis=0)
-        products(left, [ins["w"]], y_ref)
-        at = 0
-        for o in out:
-            for row in range(o.shape[0]):
-                o[row] = combine(y_ref, at, width)
-                at += 1
-
-    acc = call(
-        {**rims, **results, "skip": skip, "w": w_skip},
-        [((r,) + image[:1] + (outs,), F32) for r in skip_rows],
-        skip_body,
-        [x_scratch(r + 2) for r in skip_rows] + [y_scratch(sum(skip_rows))],
-        cost(sum(skip_rows)),
-    )
+        cases = [(lag == 1, [handed_view(ins, t)])]
+        plain = lag != 1
+        if t == 3:
+            cases.append((lag == 3, [handed_view(ins, 1)]))
+            plain = plain & (lag != 3)
+        cases += around(*rim_rows(ins, 2 + t), ins["skip"].at[t], also=plain)
+        fill(x_ref, cases, own, total)
+        products(patches(x_ref), [ins["w"]], y_ref)
+        for row in range(out[0].shape[0]):
+            out[0][row] = combine(y_ref, row, width)
+
+    acc = []
+    for t, rows in ((1, own), (2, own + 2), (3, own)):
+        used = {handed[t][0], handed[1][0]} if t == 3 else {handed[t][0]}
+        acc += call(
+            {**rims, **{n: results[n] for n in sorted(used)}, "skip": skip, "w": w_skip},
+            [((rows, width, outs), F32)],
+            lambda ins, out, scratch, t=t: skip_body(t, ins, out, scratch),
+            [x_scratch(rows + 2), y_scratch(rows)],
+            cost(rows),
+        )
 
     def dec_body(t, moved, ins, out, scratch):
         x_ref, y_ref, bias_ref, few = scratch

time: 152 us -> 153 us (level)
  the two profiles are of different devices: /device:TPU:377 before, /device:TPU:387 now
where the time goes in v1:
time: 153 us; the launch traced here: 152 us
  starting transfers between devices  75.5 us (49%)
  waiting for transfers between devices  51.2 us (33%)
  Pallas kernels  23.9 us (16%)
    ppermute x25, starting transfers between devices, send(): return lax.ppermute(value, AXES, route)  75.5 us
    ppermute x25, waiting for transfers between devices, send(): return lax.ppermute(value, AXES, route)  51.2 us
    pallas_call x14, Pallas kernels, call(): pl.pallas_call(kernel, out_shape=shapes, in_specs=[pl.BlockSpec(memory_sp...  23.9 us
  transfers between devices with their start and end apart: 25, of which 9 were waited for; matrix products, arithmetic and copies ran while one was open for 0% of the time, Pallas kernels for 14%

profile of v1, /device:TPU:387, one launch (start us, length us, event | category | flops | bytes accessed | tf_op | source)
XLA Modules:
  0.0 151.9 jit_solution(3318743864722978988)
XLA Ops:
  0.6 2.3 %collective-permute-start.14 = (bf16[9,96,384]{2,1,0:T(8,128)(2,1)}, bf16[9,96,384]{2,1,0:T(8,128)(2,1)S(1)}, u32[]{:S(2)}, u32[]{:S(2)}) collective-permute-start(bf16[9,96,384]{2,1,0:T(8,128)(2,1)} %bitcast.25), channel_id=1, source_target_pairs={{0,6},{1,7},{2,0},{3,1},{4,2},{5,3},{6,4},{7,5},{8,14},{9,15},{10,... | collective-permute-start | bytes 1990664 | tf_op jit(solution)/shard_map/ppermute | solution.py:149
  2.9 4.0 %collective-permute-start.3 = (bf16[9,48,384]{2,1,0:T(8,128)(2,1)}, bf16[9,48,384]{2,1,0:T(8,128)(2,1)S(1)}, u32[]{:S(2)}, u32[]{:S(2)}) collective-permute-start(bf16[9,48,384]{2,1,0:T(8,128)(2,1)} %bitcast.31), channel_id=1, source_target_pairs={{0,4},{1,5},{2,6},{3,7},{4,0},{5,1},{6,2},{7,3},{8,12},{9,13},{10,... | collective-permute-start | bytes 995336 | tf_op jit(solution)/shard_map/ppermute | solution.py:149
  7.0 4.8 %collective-permute-start.2 = (bf16[9,48,384]{2,1,0:T(8,128)(2,1)}, bf16[9,48,384]{2,1,0:T(8,128)(2,1)S(1)}, u32[]{:S(2)}, u32[]{:S(2)}) collective-permute-start(bf16[9,48,384]{2,1,0:T(8,128)(2,1)} %bitcast.32), channel_id=1, source_target_pairs={{0,1},{1,0},{2,3},{3,2},{4,5},{5,4},{6,7},{7,6},{8,9},{9,8},{10,11... | collective-permute-start | bytes 995336 | tf_op jit(solution)/shard_map/ppermute | solution.py:149
  11.8 3.4 %collective-permute-start.13 = (bf16[9,96,384]{2,1,0:T(8,128)(2,1)}, bf16[9,96,384]{2,1,0:T(8,128)(2,1)S(1)}, u32[]{:S(2)}, u32[]{:S(2)}) collective-permute-start(bf16[9,96,384]{2,1,0:T(8,128)(2,1)} %bitcast.26), channel_id=1, source_target_pairs={{0,2},{1,3},{2,4},{3,5},{4,6},{5,7},{6,0},{7,1},{8,10},{9,11},{10,... | collective-permute-start | bytes 1990664 | tf_op jit(solution)/shard_map/ppermute | solution.py:149
  19.2 7.6 %collective-permute-done.3.refs_0_.refs_4_ = bf16[9,48,384]{2,1,0:T(8,128)(2,1)S(1)} collective-permute-done((bf16[9,48,384]{2,1,0:T(8,128)(2,1)}, bf16[9,48,384]{2,1,0:T(8,128)(2,1)S(1)}, u32[]{:S(2)}, u32[]{:S(2)}) %collective-permute-start.3) | collective-permute-done | bytes 331808 | tf_op jit(solution)/shard_map/ppermute | solution.py:149
  26.8 4.8 %collective-permute-start.6 = (bf16[1136,384]{1,0:T(8,128)(2,1)S(1)}, bf16[1136,384]{1,0:T(8,128)(2,1)S(1)}, u32[]{:S(2)}, u32[]{:S(2)}) collective-permute-start(bf16[1136,384]{1,0:T(8,128)(2,1)S(1)} %shard_map.96), channel_id=1, source_target_pairs={{0,1},{1,0},{2,3},{3,2},{4,5},{5,4},{6,7},{7,6},{8,9},{9,8},{10,11... | collective-permute-start | bytes 2617352 | tf_op jit(solution)/shard_map/ppermute | solution.py:149
  33.6 3.4 %collective-permute-start = (bf16[11,48,384]{2,1,0:T(8,128)(2,1)S(1)}, bf16[11,48,384]{2,1,0:T(8,128)(2,1)S(1)}, u32[]{:S(2)}, u32[]{:S(2)}) collective-permute-start(bf16[11,48,384]{2,1,0:T(8,128)(2,1)S(1)} %get-tuple-element.16.refs_0_), channel_id=1, source_target_pairs={{0,2},{1,3},{2,4},{3,5},{4,6},{5,7},{6,0},{7,1},{8,10},{9,11},{10,... | collective-permute-start | bytes 1216520 | tf_op jit(solution)/shard_map/ppermute | solution.py:149
  39.2 8.6 %collective-permute-done.1.refs_2_ = bf16[11,48,384]{2,1,0:T(8,128)(2,1)S(1)} collective-permute-done((bf16[11,48,384]{2,1,0:T(8,128)(2,1)S(1)}, bf16[11,48,384]{2,1,0:T(8,128)(2,1)S(1)}, u32[]{:S(2)}, u32[]{:S(2)}) %collective-permute-start.1) | collective-permute-done | bytes 405536 | tf_op jit(solution)/shard_map/ppermute | solution.py:149
  49.8 3.4 %collective-permute-start.5 = (bf16[9,48,384]{2,1,0:T(8,128)(2,1)S(1)}, bf16[9,48,384]{2,1,0:T(8,128)(2,1)S(1)}, u32[]{:S(2)}, u32[]{:S(2)}) collective-permute-start(bf16[9,48,384]{2,1,0:T(8,128)(2,1)S(1)} %collective-permute-done.2.refs_3_), channel_id=1, source_target_pairs={{0,6},{1,7},{2,0},{3,1},{4,2},{5,3},{6,4},{7,5},{8,14},{9,15},{10,... | collective-permute-start | bytes 995336 | tf_op jit(solution)/shard_map/ppermute | solution.py:149
  55.1 4.6 %collective-permute-done.5.refs_6_ = bf16[9,48,384]{2,1,0:T(8,128)(2,1)S(1)} collective-permute-done((bf16[9,48,384]{2,1,0:T(8,128)(2,1)S(1)}, bf16[9,48,384]{2,1,0:T(8,128)(2,1)S(1)}, u32[]{:S(2)}, u32[]{:S(2)}) %collective-permute-start.5) | collective-permute-done | bytes 331808 | tf_op jit(solution)/shard_map/ppermute | solution.py:149
  60.5 12.2 %collective-permute-done.4.refs_5_ = bf16[9,48,384]{2,1,0:T(8,128)(2,1)S(1)} collective-permute-done((bf16[9,48,384]{2,1,0:T(8,128)(2,1)S(1)}, bf16[9,48,384]{2,1,0:T(8,128)(2,1)S(1)}, u32[]{:S(2)}, u32[]{:S(2)}) %collective-permute-start.4) | collective-permute-done | bytes 331808 | tf_op jit(solution)/shard_map/ppermute | solution.py:149
  72.7 3.8 %shard_map.97 = (bf16[9,64,384]{2,1,0:T(8,128)(2,1)S(1)}, bf16[9,384,384]{2,1,0:T(8,128)(2,1)S(1)}) custom-call(bf16[11,48,384]{2,1,0:T(8,128)(2,1)S(1)} %get-tuple-element.16.refs_0_, bf16[11,48,384]{2,1,0:T(8,128)(2,1)S(1)} %collective-permute-done.refs_1_, bf16[11,48,384]{2,1,0:T(8,128)(2,1)S(1)} %collective-permute-done.1.refs_2_, ...), custom_call_target="tpu_custom_call" | custom-call | flops 3057647616 | bytes 4105728 | tf_op jit(solution)/shard_map/pallas_call | solution.py:32
  76.5 4.5 %collective-permute-start.8 = (bf16[9,64,384]{2,1,0:T(8,128)(2,1)S(1)}, bf16[9,64,384]{2,1,0:T(8,128)(2,1)S(1)}, u32[]{:S(2)}, u32[]{:S(2)}) collective-permute-start(bf16[9,64,384]{2,1,0:T(8,128)(2,1)S(1)} %get-tuple-element.20.refs_6_.refs_2_.refs_1_), channel_id=1, source_target_pairs={{0,8},{1,9},{2,10},{3,11},{4,12},{5,13},{6,14},{7,15},{8,16},{9,17... | collective-permute-start | bytes 1327112 | tf_op jit(solution)/shard_map/ppermute | solution.py:149
  83.0 3.4 %collective-permute-start.17 = (bf16[9,96,384]{2,1,0:T(8,128)(2,1)S(1)}, bf16[9,96,384]{2,1,0:T(8,128)(2,1)S(1)}, u32[]{:S(2)}, u32[]{:S(2)}) collective-permute-start(bf16[9,96,384]{2,1,0:T(8,128)(2,1)S(1)} %collective-permute-done.15.refs_3_), channel_id=1, source_target_pairs={{0,2},{1,3},{2,4},{3,5},{4,6},{5,7},{6,0},{7,1},{8,10},{9,11},{10,... | collective-permute-start | bytes 1990664 | tf_op jit(solution)/shard_map/ppermute | solution.py:149
  91.3 2.5 %collective-permute-start.11 = (bf16[7,64,384]{2,1,0:T(8,128)(2,1)S(1)}, bf16[7,64,384]{2,1,0:T(8,128)(2,1)S(1)}, u32[]{:S(2)}, u32[]{:S(2)}) collective-permute-start(bf16[7,64,384]{2,1,0:T(8,128)(2,1)S(1)} %shard_map.98.refs_7_.refs_2_.refs_3_), channel_id=1, source_target_pairs={{0,8},{1,9},{2,10},{3,11},{4,12},{5,13},{6,14},{7,15},{8,16},{9,17... | collective-permute-start | bytes 1032200 | tf_op jit(solution)/shard_map/ppermute | solution.py:149
  93.8 5.3 %collective-permute-done.18.refs_6_ = bf16[9,96,384]{2,1,0:T(8,128)(2,1)S(1)} collective-permute-done((bf16[9,96,384]{2,1,0:T(8,128)(2,1)S(1)}, bf16[9,96,384]{2,1,0:T(8,128)(2,1)S(1)}, u32[]{:S(2)}, u32[]{:S(2)}) %collective-permute-start.18) | collective-permute-done | bytes 663584 | tf_op jit(solution)/shard_map/ppermute | solution.py:149
  101.1 5.3 %collective-permute-done.19.refs_7_ = bf16[9,96,384]{2,1,0:T(8,128)(2,1)S(1)} collective-permute-done((bf16[9,96,384]{2,1,0:T(8,128)(2,1)S(1)}, bf16[9,96,384]{2,1,0:T(8,128)(2,1)S(1)}, u32[]{:S(2)}, u32[]{:S(2)}) %collective-permute-start.19) | collective-permute-done | bytes 663584 | tf_op jit(solution)/shard_map/ppermute | solution.py:149
  106.4 3.4 %shard_map.102 = (bf16[5,64,384]{2,1,0:T(8,128)(2,1)S(1)}, bf16[9,384,384]{2,1,0:T(8,128)(2,1)S(1)}, bf16[9,384,384]{2,1,0:T(8,128)(2,1)S(1)}) custom-call(bf16[9,96,384]{2,1,0:T(8,128)(2,1)S(1)} %bitcast.28, bf16[9,96,384]{2,1,0:T(8,128)(2,1)S(1)} %collective-permute-done.13.refs_0_.refs_1_, ...), custom_call_target="tpu_custom_call" | custom-call | flops 3397386240 | bytes 7460352 | tf_op jit(solution)/shard_map/pallas_call | solution.py:32
  109.8 2.3 %collective-permute-start.20 = (bf16[5,64,384]{2,1,0:T(8,128)(2,1)S(1)}, bf16[5,64,384]{2,1,0:T(8,128)(2,1)S(1)}, u32[]{:S(2)}, u32[]{:S(2)}) collective-permute-start(bf16[5,64,384]{2,1,0:T(8,128)(2,1)S(1)} %get-tuple-element.24.refs_5_), channel_id=1, source_target_pairs={{8,0},{9,1},{10,2},{11,3},{12,4},{13,5},{14,6},{15,7},{16,8},{17,9... | collective-permute-start | bytes 737288 | tf_op jit(solution)/shard_map/ppermute | solution.py:149
  113.8 6.4 %collective-permute-start.12 = (bf16[5,64,384]{2,1,0:T(8,128)(2,1)S(1)}, bf16[5,64,384]{2,1,0:T(8,128)(2,1)S(1)}, u32[]{:S(2)}, u32[]{:S(2)}) collective-permute-start(bf16[5,64,384]{2,1,0:T(8,128)(2,1)S(1)} %shard_map.99.refs_8_.refs_3_.refs_1_), channel_id=1, source_target_pairs={{0,8},{1,9},{2,10},{3,11},{4,12},{5,13},{6,14},{7,15},{8,16},{9,17... | collective-permute-start | bytes 737288 | tf_op jit(solution)/shard_map/ppermute | solution.py:149
  122.6 3.9 %collective-permute-start.21 = (bf16[2,64,384]{2,1,0:T(8,128)(2,1)S(1)}, bf16[2,64,384]{2,1,0:T(8,128)(2,1)S(1)}, u32[]{:S(2)}, u32[]{:S(2)}) collective-permute-start(bf16[2,64,384]{2,1,0:T(8,128)(2,1)S(1)} %get-tuple-element.27), channel_id=1, source_target_pairs={{8,1},{9,2},{10,3},{11,4},{12,5},{13,6},{14,7},{16,9},{17,10},{18,... | collective-permute-start | bytes 294920 | tf_op jit(solution)/shard_map/ppermute | solution.py:149
  126.5 7.5 %collective-permute-start.23 = (bf16[2,64,384]{2,1,0:T(8,128)(2,1)S(1)}, bf16[2,64,384]{2,1,0:T(8,128)(2,1)S(1)}, u32[]{:S(2)}, u32[]{:S(2)}) collective-permute-start(bf16[2,64,384]{2,1,0:T(8,128)(2,1)S(1)} %get-tuple-element.29), channel_id=1, source_target_pairs={{9,0},{10,1},{11,2},{12,3},{13,4},{14,5},{15,6},{17,8},{18,9},{19,... | collective-permute-start | bytes 294920 | tf_op jit(solution)/shard_map/ppermute | solution.py:149
  137.5 3.0 %collective-permute-done.22.refs_1_ = bf16[3,64,384]{2,1,0:T(8,128)(2,1)S(1)} collective-permute-done((bf16[3,64,384]{2,1,0:T(8,128)(2,1)S(1)}, bf16[3,64,384]{2,1,0:T(8,128)(2,1)S(1)}, u32[]{:S(2)}, u32[]{:S(2)}) %collective-permute-start.22) | collective-permute-done | bytes 147488 | tf_op jit(solution)/shard_map/ppermute | solution.py:149
  147.2 2.6 %collective-permute-done.24.refs_0_ = bf16[5,64,384]{2,1,0:T(8,128)(2,1)S(1)} collective-permute-done((bf16[5,64,384]{2,1,0:T(8,128)(2,1)S(1)}, bf16[5,64,384]{2,1,0:T(8,128)(2,1)S(1)}, u32[]{:S(2)}, u32[]{:S(2)}) %collective-permute-start.24) | collective-permute-done | bytes 245792 | tf_op jit(solution)/shard_map/ppermute | solution.py:149
  (50 shorter events, 37.6 us)
Async XLA Ops:
  0.6 32.9 %collective-permute-start.14 = (bf16[9,96,384]{2,1,0:T(8,128)(2,1)}, bf16[9,96,384]{2,1,0:T(8,128)(2,1)S(1)}, u32[]{:S(2)}, u32[]{:S(2)}) collective-permute-start(bf16[9,96,384]{2,1,0:T(8,128)(2,1)} %bitcast.25), channel_id=1, source_target_pairs={{0,6},{1,7},{2,0},{3,1},{4,2},{5,3},{6,4},{7,5},{8,14},{9,15},{10,... | collective-permute-start | bytes 1990664 | tf_op jit(solution)/shard_map/ppermute | solution.py:149
  2.9 23.8 %collective-permute-start.3 = (bf16[9,48,384]{2,1,0:T(8,128)(2,1)}, bf16[9,48,384]{2,1,0:T(8,128)(2,1)S(1)}, u32[]{:S(2)}, u32[]{:S(2)}) collective-permute-start(bf16[9,48,384]{2,1,0:T(8,128)(2,1)} %bitcast.31), channel_id=1, source_target_pairs={{0,4},{1,5},{2,6},{3,7},{4,0},{5,1},{6,2},{7,3},{8,12},{9,13},{10,... | collective-permute-start | bytes 995336 | tf_op jit(solution)/shard_map/ppermute | solution.py:149
  7.0 24.6 %collective-permute-start.2 = (bf16[9,48,384]{2,1,0:T(8,128)(2,1)}, bf16[9,48,384]{2,1,0:T(8,128)(2,1)S(1)}, u32[]{:S(2)}, u32[]{:S(2)}) collective-permute-start(bf16[9,48,384]{2,1,0:T(8,128)(2,1)} %bitcast.32), channel_id=1, source_target_pairs={{0,1},{1,0},{2,3},{3,2},{4,5},{5,4},{6,7},{7,6},{8,9},{9,8},{10,11... | collective-permute-start | bytes 995336 | tf_op jit(solution)/shard_map/ppermute | solution.py:149
  11.8 25.1 %collective-permute-start.13 = (bf16[9,96,384]{2,1,0:T(8,128)(2,1)}, bf16[9,96,384]{2,1,0:T(8,128)(2,1)S(1)}, u32[]{:S(2)}, u32[]{:S(2)}) collective-permute-start(bf16[9,96,384]{2,1,0:T(8,128)(2,1)} %bitcast.26), channel_id=1, source_target_pairs={{0,2},{1,3},{2,4},{3,5},{4,6},{5,7},{6,0},{7,1},{8,10},{9,11},{10,... | collective-permute-start | bytes 1990664 | tf_op jit(solution)/shard_map/ppermute | solution.py:149
  17.2 35.9 %collective-permute-start.7 = (bf16[11,64,384]{2,1,0:T(8,128)(2,1)S(1)}, bf16[11,64,384]{2,1,0:T(8,128)(2,1)S(1)}, u32[]{:S(2)}, u32[]{:S(2)}) collective-permute-start(bf16[11,64,384]{2,1,0:T(8,128)(2,1)S(1)} %get-tuple-element.19), channel_id=1, source_target_pairs={{1,2},{2,1},{3,4},{4,3},{5,6},{6,5},{9,10},{10,9},{11,12},{12,11},... | collective-permute-start | bytes 1622024 | tf_op jit(solution)/shard_map/ppermute | solution.py:149
  26.8 45.9 %collective-permute-start.6 = (bf16[1136,384]{1,0:T(8,128)(2,1)S(1)}, bf16[1136,384]{1,0:T(8,128)(2,1)S(1)}, u32[]{:S(2)}, u32[]{:S(2)}) collective-permute-start(bf16[1136,384]{1,0:T(8,128)(2,1)S(1)} %shard_map.96), channel_id=1, source_target_pairs={{0,1},{1,0},{2,3},{3,2},{4,5},{5,4},{6,7},{7,6},{8,9},{9,8},{10,11... | collective-permute-start | bytes 2617352 | tf_op jit(solution)/shard_map/ppermute | solution.py:149
  31.6 16.2 %collective-permute-start.1 = (bf16[11,48,384]{2,1,0:T(8,128)(2,1)S(1)}, bf16[11,48,384]{2,1,0:T(8,128)(2,1)S(1)}, u32[]{:S(2)}, u32[]{:S(2)}) collective-permute-start(bf16[11,48,384]{2,1,0:T(8,128)(2,1)S(1)} %get-tuple-element.17), channel_id=1, source_target_pairs={{0,6},{1,7},{2,0},{3,1},{4,2},{5,3},{6,4},{7,5},{8,14},{9,15},{10,... | collective-permute-start | bytes 1216520 | tf_op jit(solution)/shard_map/ppermute | solution.py:149
  33.6 16.2 %collective-permute-start = (bf16[11,48,384]{2,1,0:T(8,128)(2,1)S(1)}, bf16[11,48,384]{2,1,0:T(8,128)(2,1)S(1)}, u32[]{:S(2)}, u32[]{:S(2)}) collective-permute-start(bf16[11,48,384]{2,1,0:T(8,128)(2,1)S(1)} %get-tuple-element.16.refs_0_), channel_id=1, source_target_pairs={{0,2},{1,3},{2,4},{3,5},{4,6},{5,7},{6,0},{7,1},{8,10},{9,11},{10,... | collective-permute-start | bytes 1216520 | tf_op jit(solution)/shard_map/ppermute | solution.py:149
  37.0 44.1 %collective-permute-start.15 = (bf16[9,96,384]{2,1,0:T(8,128)(2,1)S(1)}, bf16[9,96,384]{2,1,0:T(8,128)(2,1)S(1)}, u32[]{:S(2)}, u32[]{:S(2)}) collective-permute-start(bf16[9,96,384]{2,1,0:T(8,128)(2,1)S(1)} %bitcast.27), channel_id=1, source_target_pairs={{0,1},{1,0},{2,3},{3,2},{4,5},{5,4},{6,7},{7,6},{8,9},{9,8},{10,11... | collective-permute-start | bytes 1990664 | tf_op jit(solution)/shard_map/ppermute | solution.py:149
  47.8 38.5 %collective-permute-start.16 = (bf16[9,96,384]{2,1,0:T(8,128)(2,1)S(1)}, bf16[9,96,384]{2,1,0:T(8,128)(2,1)S(1)}, u32[]{:S(2)}, u32[]{:S(2)}) collective-permute-start(bf16[9,96,384]{2,1,0:T(8,128)(2,1)S(1)} %shard_map.101), channel_id=1, source_target_pairs={{0,2},{1,7},{2,4},{3,1},{4,6},{5,3},{6,0},{7,5},{8,10},{9,15},{10,... | collective-permute-start | bytes 1990664 | tf_op jit(solution)/shard_map/ppermute | solution.py:149
  49.8 9.9 %collective-permute-start.5 = (bf16[9,48,384]{2,1,0:T(8,128)(2,1)S(1)}, bf16[9,48,384]{2,1,0:T(8,128)(2,1)S(1)}, u32[]{:S(2)}, u32[]{:S(2)}) collective-permute-start(bf16[9,48,384]{2,1,0:T(8,128)(2,1)S(1)} %collective-permute-done.2.refs_3_), channel_id=1, source_target_pairs={{0,6},{1,7},{2,0},{3,1},{4,2},{5,3},{6,4},{7,5},{8,14},{9,15},{10,... | collective-permute-start | bytes 995336 | tf_op jit(solution)/shard_map/ppermute | solution.py:149
  53.2 19.5 %collective-permute-start.4 = (bf16[9,48,384]{2,1,0:T(8,128)(2,1)S(1)}, bf16[9,48,384]{2,1,0:T(8,128)(2,1)S(1)}, u32[]{:S(2)}, u32[]{:S(2)}) collective-permute-start(bf16[9,48,384]{2,1,0:T(8,128)(2,1)S(1)} %collective-permute-done.2.refs_3_), channel_id=1, source_target_pairs={{0,2},{1,3},{2,4},{3,5},{4,6},{5,7},{6,0},{7,1},{8,10},{9,11},{10,... | collective-permute-start | bytes 995336 | tf_op jit(solution)/shard_map/ppermute | solution.py:149
  59.7 28.6 %collective-permute-start.9 = (bf16[6,64,384]{2,1,0:T(8,128)(2,1)S(1)}, bf16[6,64,384]{2,1,0:T(8,128)(2,1)S(1)}, u32[]{:S(2)}, u32[]{:S(2)}) collective-permute-start(bf16[6,64,384]{2,1,0:T(8,128)(2,1)S(1)} %get-tuple-element.21), channel_id=1, source_target_pairs={{0,1},{1,0},{2,3},{3,2},{4,5},{5,4},{6,7},{7,6}} | collective-permute-start | bytes 884744 | tf_op jit(solution)/shard_map/ppermute | solution.py:149
  76.5 12.5 %collective-permute-start.8 = (bf16[9,64,384]{2,1,0:T(8,128)(2,1)S(1)}, bf16[9,64,384]{2,1,0:T(8,128)(2,1)S(1)}, u32[]{:S(2)}, u32[]{:S(2)}) collective-permute-start(bf16[9,64,384]{2,1,0:T(8,128)(2,1)S(1)} %get-tuple-element.20.refs_6_.refs_2_.refs_1_), channel_id=1, source_target_pairs={{0,8},{1,9},{2,10},{3,11},{4,12},{5,13},{6,14},{7,15},{8,16},{9,17... | collective-permute-start | bytes 1327112 | tf_op jit(solution)/shard_map/ppermute | solution.py:149
  81.0 18.1 %collective-permute-start.18 = (bf16[9,96,384]{2,1,0:T(8,128)(2,1)S(1)}, bf16[9,96,384]{2,1,0:T(8,128)(2,1)S(1)}, u32[]{:S(2)}, u32[]{:S(2)}) collective-permute-start(bf16[9,96,384]{2,1,0:T(8,128)(2,1)S(1)} %collective-permute-done.15.refs_3_), channel_id=1, source_target_pairs={{0,6},{1,7},{2,0},{3,1},{4,2},{5,3},{6,4},{7,5},{8,14},{9,15},{10,... | collective-permute-start | bytes 1990664 | tf_op jit(solution)/shard_map/ppermute | solution.py:149
  83.0 18.1 %collective-permute-start.17 = (bf16[9,96,384]{2,1,0:T(8,128)(2,1)S(1)}, bf16[9,96,384]{2,1,0:T(8,128)(2,1)S(1)}, u32[]{:S(2)}, u32[]{:S(2)}) collective-permute-start(bf16[9,96,384]{2,1,0:T(8,128)(2,1)S(1)} %collective-permute-done.15.refs_3_), channel_id=1, source_target_pairs={{0,2},{1,3},{2,4},{3,5},{4,6},{5,7},{6,0},{7,1},{8,10},{9,11},{10,... | collective-permute-start | bytes 1990664 | tf_op jit(solution)/shard_map/ppermute | solution.py:149
  86.4 20.0 %collective-permute-start.19 = (bf16[9,96,384]{2,1,0:T(8,128)(2,1)S(1)}, bf16[9,96,384]{2,1,0:T(8,128)(2,1)S(1)}, u32[]{:S(2)}, u32[]{:S(2)}) collective-permute-start(bf16[9,96,384]{2,1,0:T(8,128)(2,1)S(1)} %collective-permute-done.16.refs_4_), channel_id=1, source_target_pairs={{0,1},{1,0},{2,3},{3,2},{4,5},{5,4},{6,7},{7,6},{8,9},{9,8},{10,11... | collective-permute-start | bytes 1990664 | tf_op jit(solution)/shard_map/ppermute | solution.py:149
  91.3 20.8 %collective-permute-start.11 = (bf16[7,64,384]{2,1,0:T(8,128)(2,1)S(1)}, bf16[7,64,384]{2,1,0:T(8,128)(2,1)S(1)}, u32[]{:S(2)}, u32[]{:S(2)}) collective-permute-start(bf16[7,64,384]{2,1,0:T(8,128)(2,1)S(1)} %shard_map.98.refs_7_.refs_2_.refs_3_), channel_id=1, source_target_pairs={{0,8},{1,9},{2,10},{3,11},{4,12},{5,13},{6,14},{7,15},{8,16},{9,17... | collective-permute-start | bytes 1032200 | tf_op jit(solution)/shard_map/ppermute | solution.py:149
  109.8 11.6 %collective-permute-start.20 = (bf16[5,64,384]{2,1,0:T(8,128)(2,1)S(1)}, bf16[5,64,384]{2,1,0:T(8,128)(2,1)S(1)}, u32[]{:S(2)}, u32[]{:S(2)}) collective-permute-start(bf16[5,64,384]{2,1,0:T(8,128)(2,1)S(1)} %get-tuple-element.24.refs_5_), channel_id=1, source_target_pairs={{8,0},{9,1},{10,2},{11,3},{12,4},{13,5},{14,6},{15,7},{16,8},{17,9... | collective-permute-start | bytes 737288 | tf_op jit(solution)/shard_map/ppermute | solution.py:149
  113.8 31.3 %collective-permute-start.12 = (bf16[5,64,384]{2,1,0:T(8,128)(2,1)S(1)}, bf16[5,64,384]{2,1,0:T(8,128)(2,1)S(1)}, u32[]{:S(2)}, u32[]{:S(2)}) collective-permute-start(bf16[5,64,384]{2,1,0:T(8,128)(2,1)S(1)} %shard_map.99.refs_8_.refs_3_.refs_1_), channel_id=1, source_target_pairs={{0,8},{1,9},{2,10},{3,11},{4,12},{5,13},{6,14},{7,15},{8,16},{9,17... | collective-permute-start | bytes 737288 | tf_op jit(solution)/shard_map/ppermute | solution.py:149
  122.6 14.9 %collective-permute-start.21 = (bf16[2,64,384]{2,1,0:T(8,128)(2,1)S(1)}, bf16[2,64,384]{2,1,0:T(8,128)(2,1)S(1)}, u32[]{:S(2)}, u32[]{:S(2)}) collective-permute-start(bf16[2,64,384]{2,1,0:T(8,128)(2,1)S(1)} %get-tuple-element.27), channel_id=1, source_target_pairs={{8,1},{9,2},{10,3},{11,4},{12,5},{13,6},{14,7},{16,9},{17,10},{18,... | collective-permute-start | bytes 294920 | tf_op jit(solution)/shard_map/ppermute | solution.py:149
  126.5 11.0 %collective-permute-start.23 = (bf16[2,64,384]{2,1,0:T(8,128)(2,1)S(1)}, bf16[2,64,384]{2,1,0:T(8,128)(2,1)S(1)}, u32[]{:S(2)}, u32[]{:S(2)}) collective-permute-start(bf16[2,64,384]{2,1,0:T(8,128)(2,1)S(1)} %get-tuple-element.29), channel_id=1, source_target_pairs={{9,0},{10,1},{11,2},{12,3},{13,4},{14,5},{15,6},{17,8},{18,9},{19,... | collective-permute-start | bytes 294920 | tf_op jit(solution)/shard_map/ppermute | solution.py:149
  134.1 6.5 %collective-permute-start.22 = (bf16[3,64,384]{2,1,0:T(8,128)(2,1)S(1)}, bf16[3,64,384]{2,1,0:T(8,128)(2,1)S(1)}, u32[]{:S(2)}, u32[]{:S(2)}) collective-permute-start(bf16[3,64,384]{2,1,0:T(8,128)(2,1)S(1)} %get-tuple-element.28.refs_6_), channel_id=1, source_target_pairs={{8,0},{9,1},{10,2},{11,3},{12,4},{13,5},{14,6},{15,7},{16,8},{17,9... | collective-permute-start | bytes 442376 | tf_op jit(solution)/shard_map/ppermute | solution.py:149
  142.3 7.5 %collective-permute-start.24 = (bf16[5,64,384]{2,1,0:T(8,128)(2,1)S(1)}, bf16[5,64,384]{2,1,0:T(8,128)(2,1)S(1)}, u32[]{:S(2)}, u32[]{:S(2)}) collective-permute-start(bf16[5,64,384]{2,1,0:T(8,128)(2,1)S(1)} %shard_map.106.refs_7_), channel_id=1, source_target_pairs={{8,0},{9,1},{10,2},{11,3},{12,4},{13,5},{14,6},{15,7},{16,8},{17,9... | collective-permute-start | bytes 737288 | tf_op jit(solution)/shard_map/ppermute | solution.py:149
  (6 other events, 158.5 us)
